TPU v7x, 32 devices: a whole 2x2x4 slice. The times are simulated.
32 devices in a mesh: member: 2 (over core), shard: 16 (over z, y, x).
Axes of the slice: x: 2, y: 2, z: 4, core: 2. Of those that a mesh axis runs over, the one named last changes fastest.
Arguments:
- layer_input: bfloat16 [2, 180, 5120], P('member', None, 'shard'), may hold values from -6 to 6
- norm_gain: float32 [2, 5120], P('member'), may hold values from 0.5 to 2
- w_gate: bfloat16 [2, 5120, 1792], P('member', None, 'shard'), may hold values from -0.0559017 to 0.0559017
- w_up: bfloat16 [2, 5120, 1792], P('member', None, 'shard'), may hold values from -0.0559017 to 0.0559017
- hidden_cot: bfloat16 [2, 180, 1792], P('member', None, 'shard'), may hold values from -3 to 5
- output_cot: bfloat16 [2, 180, 5120], P('member', None, 'shard'), may hold values from -6 to 6
- embed: bfloat16 [2, 4096, 5120], P('member', 'shard'), may hold values from -0.078125 to 0.078125
- suffix_ids: int32 [180], replicated, may hold values from 0 to 4095
Outputs:
- delta: float32 [180, 4096], P(None, 'shard')
All inputs are finite; a program needn't handle non-finite values.
Results may differ from a plain program's by a relative error of at most 0.0047.
Values may be sent and summed in bfloat16 or wider, within the bound.
A program may use at most 64 MiB of HBM per device.

v0:
```python
import jax
import jax.numpy as jnp
from jax import lax
from jax.sharding import PartitionSpec as P


def on_device(layer_input, norm_gain, w_gate, w_up, hidden_cot, output_cot, embed, suffix_ids):
    input_local = layer_input[0]
    cot_local = output_cot[0]
    gain = norm_gain[0]
    gate_w = w_gate[0]
    up_w = w_up[0]
    table = embed[0]
    whole_input = lax.all_gather(input_local, "shard", axis=1, tiled=True)
    inputs = whole_input.astype(jnp.float32)
    width = inputs.shape[1]
    inv_rms = 1.0 / jnp.sqrt(jnp.mean(inputs * inputs, axis=1, keepdims=True) + 1e-05)
    normed = (inputs * inv_rms * gain[None, :]).astype(jnp.bfloat16)
    gate_pre = jnp.dot(normed, gate_w, preferred_element_type=jnp.float32)
    up_proj = jnp.dot(normed, up_w, preferred_element_type=jnp.float32)
    sigmoid_gate = jax.nn.sigmoid(gate_pre)
    hid_f = hidden_cot[0].astype(jnp.float32)
    gate_grad = (hid_f * up_proj * sigmoid_gate * (1.0 + gate_pre * (1.0 - sigmoid_gate))).astype(
        jnp.bfloat16
    )
    up_grad = (hid_f * gate_pre * sigmoid_gate).astype(jnp.bfloat16)
    contract = (((1,), (1,)), ((), ()))
    share_width = input_local.shape[1]
    part = lax.dot_general(gate_w, gate_grad, contract, preferred_element_type=jnp.float32)
    share_t = lax.psum_scatter(
        part + lax.dot_general(up_w, up_grad, contract, preferred_element_type=jnp.float32),
        "shard",
        scatter_dimension=0,
        tiled=True,
    )
    share = share_t.T
    offset = lax.axis_index("shard") * share_width
    gain_share = lax.dynamic_slice_in_dim(gain, offset, share_width, 0)
    input_share = input_local.astype(jnp.float32)
    scaled = share * gain_share[None, :]
    partial_proj = jnp.sum(input_share * scaled, axis=1)
    proj = lax.psum(partial_proj, "shard")[:, None] / width
    grad_share = cot_local.astype(jnp.float32) + inv_rms * scaled - input_share * inv_rms**3 * proj
    grad_share = grad_share.astype(jnp.bfloat16)
    scores = lax.dot_general(
        lax.all_gather(grad_share, "shard", axis=1, tiled=True),
        table,
        contract,
        preferred_element_type=jnp.float32,
    )
    vocab_local = table.shape[0]
    first_entry = lax.axis_index("shard") * vocab_local
    entries = first_entry + lax.broadcasted_iota(jnp.int32, (1, vocab_local), 1)
    own_mask = (suffix_ids[:, None] == entries).astype(jnp.float32)
    own_local = jnp.sum(scores * own_mask, axis=1)
    current = lax.psum(own_local, "shard")
    delta = lax.psum(scores - current[:, None], "member")
    return delta


def solution(mesh):
    placed = (
        P("member", None, "shard"),
        P("member", None),
        P("member", None, "shard"),
        P("member", None, "shard"),
        P("member", None, "shard"),
        P("member", None, "shard"),
        P("member", "shard", None),
        P(),
    )
    return jax.shard_map(
        on_device, mesh=mesh, in_specs=placed, out_specs=P(None, "shard"), check_vma=False
    )
```

profile of v0, /device:TPU:0, one launch (start us, length us, event | category | flops | bytes accessed | tf_op | source)
XLA Modules:
  0.0 417.3 jit_solution(5285484548928964807)
XLA Ops:
  6.5 0.0 copy-start
  6.5 0.0 all-gather.5.cloned.1.call-start
  6.5 2.0 copy.12
  8.5 0.0 all-gather.5.cloned.1.call-update
  8.6 0.0 reduce-scatter.4.cloned.1.call-start
  8.6 88.6 %all-gather.5.cloned.1.call-done = bf16[1,180,5120]{1,0,2:T(2,128)(2,1)} async-done(((bf16[1,180,320]{1,0,2:T(2,128)(2,1)}), bf16[1,180,5120]{1,0,2:T(2,128)(2,1)}) %all-gather.5.cloned.1.call-update) | async-done | bytes 1843216 | tf_op jit(solution)/shard_map/all_gather | solution.py:14
  97.2 0.0 copy-start.5
  97.2 11.0 %copy.13 = bf16[1,180,5120]{2,1,0:T(8,128)(2,1)} copy(bf16[1,180,5120]{1,0,2:T(2,128)(2,1)} %all-gather.5.cloned.1.call-done) | data formatting | bytes 3686400 | tf_op jit(solution)/shard_map/all_gather | solution.py:14
  108.2 0.0 copy-start.1
  108.2 2.1 fusion.1
  110.3 0.0 copy-done.5
  110.3 0.0 copy-done.1
  110.3 0.0 copy-start.3
  110.3 2.1 fusion.8
  112.4 0.0 copy-done.3
  112.5 6.2 %fusion.6 = f32[180,5120]{1,0:T(8,128)} fusion(bf16[1,5120,112]{1,2,0:T(8,128)(2,1)} %param.10, bf16[1,5120,112]{1,2,0:T(8,128)(2,1)} %param.11, bf16[1,180,5120]{2,1,0:T(8,128)(2,1)} %copy.13, f32[5120]{0:T(1024)S(1)} %bitcast.68, f32[180]{0:T(256)S(1)} %get-tuple-element.6, f32[180,112]{1,0:T(8,128)S(1)} %fusion.8, bf16[1,180,112]{2,1,0:T(8,128)(2,1)S(1)} %copy-done.3), kind=kOutput, calls=%fused_computation.9 | convolution fusion | flops 416784960 | bytes 7965520 | tf_op jit(solution)/shard_map/dot_general | solution.py:29
  118.7 4.9 %fusion = f32[5120,180]{0,1:T(8,128)} fusion(f32[180,5120]{1,0:T(8,128)} %fusion.6, bf16[1,5120,112]{1,2,0:T(8,128)(2,1)} %param.11, f32[180,112]{1,0:T(8,128)S(1)} %fusion.8, bf16[1,180,112]{2,1,0:T(8,128)(2,1)S(1)} %copy-done.3), kind=kOutput, calls=%fused_computation.1 | convolution fusion | flops 207501120 | bytes 8640640 | tf_op jit(solution)/shard_map/dot_general | solution.py:31
  123.6 5.6 %copy.15 = f32[5120,180]{1,0:T(8,128)} copy(f32[5120,180]{0,1:T(8,128)} %fusion) | data formatting | bytes 7372800
  129.2 0.0 copy-start.2
  129.2 0.0 copy-start.4
  129.2 0.0 reduce-scatter.4.cloned.1.call-update
  129.3 0.0 all-gather.7.cloned.1.call-start
  129.3 0.1 dynamic-slice_reduce_fusion
  129.4 114.3 %reduce-scatter.4.cloned.1.call-done = f32[320,180]{1,0:T(8,128)} async-done(((f32[5120,180]{1,0:T(8,128)}), f32[320,180]{1,0:T(8,128)}) %reduce-scatter.4.cloned.1.call-update) | async-done | bytes 230416
  243.7 1.1 copy.16
  244.9 0.0 copy-done.2
  244.9 0.1 fusion.33
  245.0 41.3 %psum.21 = f32[180]{0:T(256)S(1)} all-reduce(f32[180]{0:T(256)S(1)} %fusion.33), channel_id=1, replica_groups=mesh['member'=2,'shard'=16] {'shard'}, use_global_device_ids=true, to_apply=%region_3.0 | all-reduce | flops 180 | bytes 1440 | tf_op jit(solution)/shard_map/psum | solution.py:42
  286.3 0.0 copy-done.4
  286.3 0.8 fusion.34
  287.1 0.0 all-gather.7.cloned.1.call-update
  287.1 0.0 all-reduce.2.cloned.1.call-start
  287.2 57.4 %all-gather.7.cloned.1.call-done = bf16[16,320,180]{1,2,0:T(8,128)(2,1)} async-done(((bf16[1,320,180]{1,2,0:T(8,128)(2,1)}), bf16[16,320,180]{1,2,0:T(8,128)(2,1)}) %all-gather.7.cloned.1.call-update) | async-done | bytes 1843216 | tf_op jit(solution)/shard_map/all_gather | solution.py:46
  344.6 3.3 copy.14
  347.9 0.0 copy-start.6
  347.9 4.5 %reshape.35 = bf16[5120,180]{0,1:T(8,128)(2,1)} reshape(bf16[16,320,180]{1,0,2:T(8,128)(2,1)} %copy.14) | data formatting | bytes 3686400
  352.5 0.0 copy-done
  352.5 0.0 copy-done.6
  352.5 2.6 select_reduce_fusion
  355.1 39.2 %psum.22 = f32[180]{0:T(256)S(1)} all-reduce(f32[180]{0:T(256)S(1)} %get-tuple-element.7), channel_id=1, replica_groups=mesh['member'=2,'shard'=16] {'shard'}, use_global_device_ids=true, to_apply=%region_5.0 | all-reduce | flops 180 | bytes 1440 | tf_op jit(solution)/shard_map/psum | solution.py:56
  394.3 0.8 broadcast_subtract_fusion
  395.1 0.0 all-reduce.2.cloned.1.call-update
  395.1 14.1 %all-reduce.2.cloned.1.call-done = f32[180,256]{1,0:T(8,128)} async-done(((f32[180,256]{1,0:T(8,128)}), f32[180,256]{1,0:T(8,128)}) %all-reduce.2.cloned.1.call-update) | async-done | bytes 184336 | tf_op jit(solution)/shard_map/psum | solution.py:57
  409.2 1.6 copy.18
  (3 shorter events, 0.0 us)
Async XLA Ops:
  6.5 345.9 %copy-start = (bf16[1,256,5120]{2,1,0:T(8,128)(2,1)S(1)}, bf16[1,256,5120]{2,1,0:T(8,128)(2,1)}, u32[]{:S(2)}) copy-start(bf16[1,256,5120]{2,1,0:T(8,128)(2,1)} %param.14) | copy-start | bytes 7864324
  6.5 90.6 %all-gather.5.cloned.1.call-start = ((), (), s32[]{:S(2)}) async-start(), calls=%async_computation.2 | async-start | bytes 5570560 | tf_op jit(solution)/shard_map/all_gather | solution.py:14
  8.6 235.2 %reduce-scatter.4.cloned.1.call-start = ((), (), s32[]{:S(2)}) async-start(), calls=%async_computation.4 | async-start | bytes 5570560
  97.2 13.1 %copy-start.5 = (f32[1,5120]{1,0:T(1,128)S(1)}, f32[1,5120]{1,0:T(1,128)}, u32[]{:S(2)}) copy-start(f32[1,5120]{1,0:T(1,128)} %param.9) | copy-start | bytes 61444
  108.2 2.1 copy-start.1
  110.3 2.1 copy-start.3
  129.2 115.6 %copy-start.2 = (bf16[1,180,320]{2,1,0:T(8,128)(2,1)S(1)}, bf16[1,180,320]{2,1,0:T(8,128)(2,1)}, u32[]{:S(2)}) copy-start(bf16[1,180,320]{2,1,0:T(8,128)(2,1)} %param.8) | copy-start | bytes 345604
  129.2 157.0 %copy-start.4 = (bf16[1,180,320]{2,1,0:T(8,128)(2,1)S(1)}, bf16[1,180,320]{2,1,0:T(8,128)(2,1)}, u32[]{:S(2)}) copy-start(bf16[1,180,320]{2,1,0:T(8,128)(2,1)} %param.13) | copy-start | bytes 345604
  129.3 215.4 %all-gather.7.cloned.1.call-start = ((), (), s32[]{:S(2)}) async-start(), calls=%async_computation.3 | async-start | bytes 2402304 | tf_op jit(solution)/shard_map/all_gather | solution.py:46
  287.1 122.0 %all-reduce.2.cloned.1.call-start = ((), (), s32[]{:S(2)}) async-start(), calls=%async_computation.1 | async-start | bytes 376832 | tf_op jit(solution)/shard_map/psum | solution.py:57
  347.9 4.5 %copy-start.6 = (s32[180]{0:T(256)S(1)}, s32[180]{0:T(256)}, u32[]{:S(2)}) copy-start(s32[180]{0:T(256)} %param.15) | copy-start | bytes 2164
Sparse Core Ops, SparseCore 0:
  10.1 87.0 all-gather.4
  129.4 114.3 reduce-scatter.3
  287.3 57.3 all-gather.6
  395.2 13.8 all-reduce.1
where the time goes:
time: 418 us; the launch traced here: 417 us
  waiting for transfers between devices  274 us (66%)
  blocking collectives  80.5 us (19%)
  local copies, waits for them, and re-layouts  29.3 us (7%)
  matrix products  15.9 us (4%)
  between operations  13.2 us (3%)
    unnamed x5, waiting for transfers between devices  114 us
    all_gather x1, waiting for transfers between devices, on_device(): whole_input = lax.all_gather(input_local, 'shard', axis=1, tiled=True)  88.6 us
    all_gather x1, waiting for transfers between devices, on_device(): lax.all_gather(grad_share, 'shard', axis=1, tiled=True)  57.4 us
    psum x1, blocking collectives, on_device(): proj = lax.psum(partial_proj, 'shard')[:, None] / width  41.3 us
    psum x1, blocking collectives, on_device(): current = lax.psum(own_local, 'shard')  39.2 us
    unnamed x19, local copies, waits for them, and re-layouts  14.9 us
    psum x1, waiting for transfers between devices, on_device(): delta = lax.psum(scores - current[:, None], 'member')  14.1 us
    all_gather x1, local copies, waits for them, and re-layouts, on_device(): whole_input = lax.all_gather(input_local, 'shard', axis=1, tiled=True)  11 us
  transfers between devices with their start and end apart: 4, of which 4 were waited for; matrix products, arithmetic and copies ran while one was open for 0% of the time, Pallas kernels for 0%

commit v1 on v0

v1 whole, which is shorter than its diff:
```python
import functools

import jax
import jax.numpy as jnp
from jax import lax
from jax.experimental import pallas as pl
from jax.experimental.pallas import tpu as pltpu
from jax.sharding import PartitionSpec as P

F32 = jnp.float32
BF16 = jnp.bfloat16
NT = (((1,), (1,)), ((), ()))
TN = (((0,), (0,)), ((), ()))
HIGH = lax.Precision.HIGHEST


def grid_of(n):
    inner = 1
    while (2 * inner) ** 3 <= n:
        inner *= 2
    return n // (inner * inner), inner, inner


def kernel(
    n, members, lines, rows, width,
    x_in, gain_in, hid_in, cot_in, ids_in, wg_hbm, wu_hbm, emb_hbm, out_ref,
    xg, gg, part, r1y, r1x, r2x, r2y, r3, st_in, st_sq, st_pr, st_cu,
    wg_v, wu_v, wcat, emb_v, emb3, gain3, hcat, acc, inv_ref, sums, scores, others,
    load_sem, st_send, st_recv, x_send, x_recv, g_send, g_recv,
    s1y, q1y, s1x, q1x, s2, q2x, q2y, s3, q3, m_send, m_recv,
):
    A, B, C = lines
    rp, dl = xg.shape[1], xg.shape[2]
    half = rp // 2
    fl = hid_in.shape[1]
    fp = hcat.shape[1] // 2
    vl = emb_hbm.shape[0]
    me = lax.axis_index("shard")
    mine = lax.axis_index("member")
    c0 = lax.rem(me, C)
    b0 = lax.rem(lax.div(me, C), B)
    a0 = lax.div(me, B * C)

    def at(a, b, c):
        return (a * B + b) * C + c

    def turn(v, d, size):
        return lax.rem(v + d, size)

    def remote(src, dst, send, recv, peer, axis="shard"):
        return pltpu.make_async_remote_copy(
            src_ref=src, dst_ref=dst, send_sem=send, recv_sem=recv,
            device_id={axis: peer}, device_id_type=pl.DeviceIdType.MESH,
        )

    loads = [
        pltpu.make_async_copy(wg_hbm, wg_v, load_sem.at[0]),
        pltpu.make_async_copy(wu_hbm, wu_v, load_sem.at[1]),
        pltpu.make_async_copy(emb_hbm, emb_v, load_sem.at[2]),
    ]
    for load in loads:
        load.start()

    barrier = pltpu.get_barrier_semaphore()
    for d in range(1, n):
        pl.semaphore_signal(barrier, inc=1, device_id={"shard": turn(me, d, n)},
                            device_id_type=pl.DeviceIdType.MESH)
    for d in range(1, members):
        pl.semaphore_signal(barrier, inc=1, device_id={"member": turn(mine, d, members)},
                            device_id_type=pl.DeviceIdType.MESH)

    xg[me] = jnp.zeros((rp, dl), BF16)
    xg[me, 0:rows, :] = x_in[...]
    x_own = x_in[...].astype(F32)

    def first_row(k):
        return (lax.broadcasted_iota(jnp.int32, (8, k), 0) == 0).astype(F32)

    def to_row(values):
        return lax.dot_general(first_row(values.shape[1]), values, NT, precision=HIGH,
                               preferred_element_type=F32)

    def to_column(row, lanes):
        return lax.dot_general(row, jnp.ones((8, lanes), F32), TN, precision=HIGH,
                               preferred_element_type=F32)

    def stat_copy(k, buf, d):
        return remote(st_in.at[k], buf.at[me], st_send.at[k, d], st_recv.at[k, me], turn(me, d, n))

    def stat_send(k, buf):
        for d in range(1, n):
            stat_copy(k, buf, d).start()

    def stat_sum(k, buf):
        total = st_in[k]
        for d in range(1, n):
            src = turn(me, d, n)
            remote(st_in.at[k], buf.at[src], st_send.at[k, d], st_recv.at[k, src], src).wait_recv()
            total = total + buf[src]
        for d in range(1, n):
            stat_copy(k, buf, d).wait_send()
        return total

    pad = jnp.zeros((rp - rows, dl), F32)
    st_in[0] = to_row(jnp.concatenate([x_own * x_own, pad], axis=0))
    pl.semaphore_wait(barrier, n - 1 + members - 1)

    def gather(buf, send, recv, before, process):
        per = (B - 1) + (C - 1) + 2 * (B - 1) * (C - 1)

        def line(blk, index, peer):
            return remote(buf.at[blk], buf.at[blk], send.at[index], recv.at[blk, 0], peer)

        def piece(blk, index, peer, h):
            view = buf.at[blk, pl.ds(h * half, half)]
            return remote(view, view, send.at[index], recv.at[blk, h], peer)

        def outs(da):
            a = turn(a0, da, A)
            base = (A - 1) + da * per
            full, low, high = [], [], []
            k = 0
            for db in range(1, B):
                full.append(line(at(a, b0, c0), base + k, at(a0, turn(b0, db, B), c0)))
                k += 1
            for dc in range(1, C):
                full.append(line(at(a, b0, c0), base + k, at(a0, b0, turn(c0, dc, C))))
                k += 1
            for dc in range(1, C):
                for db in range(1, B):
                    low.append(piece(at(a, b0, turn(c0, dc, C)), base + k,
                                     at(a0, turn(b0, db, B), c0), 0))
                    k += 1
            for db in range(1, B):
                for dc in range(1, C):
                    high.append(piece(at(a, turn(b0, db, B), c0), base + k,
                                      at(a0, b0, turn(c0, dc, C)), 1))
                    k += 1
            return full, low, high

        def outer(da):
            return line(me, da - 1, at(turn(a0, da, A), b0, c0))

        for copy in outs(0)[0]:
            copy.start()
        for da in range(1, A):
            outer(da).start()
        before()

        def step(t, carry):
            @pl.when(jnp.logical_and(t >= 1, t < A))
            def _():
                src = at(turn(a0, t, A), b0, c0)
                line(src, 0, src).wait_recv()
                for copy in outs(t)[0]:
                    copy.start()

            @pl.when(jnp.logical_and(t >= 1, t < A + 1))
            def _():
                da = t - 1
                a = turn(a0, da, A)
                _, low, high = outs(da)
                xs = [at(a, b0, turn(c0, dc, C)) for dc in range(1, C)]
                ys = [at(a, turn(b0, db, B), c0) for db in range(1, B)]
                for i, blk in enumerate(xs):
                    line(blk, 0, at(a0, b0, turn(c0, i + 1, C))).wait_recv()
                    for copy in low[i * (B - 1):(i + 1) * (B - 1)]:
                        copy.start()
                for i, blk in enumerate(ys):
                    line(blk, 0, at(a0, turn(b0, i + 1, B), c0)).wait_recv()
                    for copy in high[i * (C - 1):(i + 1) * (C - 1)]:
                        copy.start()
                for blk in [at(a, b0, c0)] + xs + ys:
                    process(blk)

            @pl.when(t >= 2)
            def _():
                a = turn(a0, t - 2, A)
                for db in range(1, B):
                    for dc in range(1, C):
                        b, c = turn(b0, db, B), turn(c0, dc, C)
                        piece(at(a, b, c), 0, at(a0, b, c0), 0).wait_recv()
                        piece(at(a, b, c), 0, at(a0, b0, c), 1).wait_recv()
                        process(at(a, b, c))

            return carry

        lax.fori_loop(0, A + 2, step, 0)

        for da in range(1, A):
            outer(da).wait_send()

        def done(da, carry):
            full, low, high = outs(da)
            for copy in full + low + high:
                copy.wait_send()
            return carry

        lax.fori_loop(0, A, done, 0)

    stat_send(0, st_sq)

    def prepare():
        for b in range(n):
            gain3[b] = gain_in[:, b * dl:(b + 1) * dl]
        wcat[...] = jnp.zeros_like(wcat)
        loads[0].wait()
        wcat[:, 0:fl] = wg_v[...]
        loads[1].wait()
        wcat[:, fp:fp + fl] = wu_v[...]
        acc[...] = jnp.zeros_like(acc)
        scores[...] = jnp.zeros_like(scores)
        square = to_column(stat_sum(0, st_sq), 128)
        inv_ref[...] = 1.0 / jnp.sqrt(square / width + 1e-05)

    def up(blk):
        x = xg[blk].astype(F32)
        normed = (x * inv_ref[:, 0:1] * gain3[blk]).astype(BF16)
        w = wcat[pl.ds(pl.multiple_of(blk * dl, dl), dl), :]
        acc[...] += jnp.dot(normed, w, preferred_element_type=F32)

    gather(xg, x_send, x_recv, prepare, up)

    gate_pre = acc[0:rows, 0:fl]
    up_proj = acc[0:rows, fp:fp + fl]
    hid = hid_in[...].astype(F32)
    s = jax.nn.sigmoid(gate_pre)
    gate_grad = (hid * up_proj * s * (1.0 + gate_pre * (1.0 - s))).astype(BF16)
    up_grad = (hid * gate_pre * s).astype(BF16)
    hcat[...] = jnp.zeros_like(hcat)
    hcat[0:rows, 0:fl] = gate_grad
    hcat[0:rows, fp:fp + fl] = up_grad
    st_in[1] = to_row(hcat[...].astype(F32) * acc[...])
    stat_send(1, st_pr)

    def product(blk):
        w = wcat[pl.ds(pl.multiple_of(blk * dl, dl), dl), :]
        return lax.dot_general(hcat[...], w, NT, preferred_element_type=F32)

    lo, hi = pl.ds(0, half), pl.ds(half, half)

    def first(a):
        copies = []
        for db in range(1, B):
            for dc in range(1, C):
                b, c = turn(b0, db, B), turn(c0, dc, C)
                blk = at(a, b, c)
                copies.append((blk, remote(part.at[blk, lo], r1y.at[a, c, b0],
                                           s1y.at[blk], q1y.at[a, c, b0], at(a0, b, c0))))
                copies.append((blk, remote(part.at[blk, hi], r1x.at[a, b, c0],
                                           s1x.at[blk], q1x.at[a, b, c0], at(a0, b0, c))))
        return copies

    def second(a):
        copies = []
        for dc in range(1, C):
            c = turn(c0, dc, C)
            blk = at(a, b0, c)
            copies.append((blk, c, 0, remote(part.at[blk], r2x.at[a, c0], s2.at[blk],
                                             q2x.at[a, c0], at(a0, b0, c))))
        for db in range(1, B):
            b = turn(b0, db, B)
            blk = at(a, b, c0)
            copies.append((blk, b, 1, remote(part.at[blk], r2y.at[a, b0], s2.at[blk],
                                             q2y.at[a, b0], at(a0, b, c0))))
        return copies

    def third(a):
        blk = at(a, b0, c0)
        return remote(part.at[blk], r3.at[a0], s3.at[a], q3.at[a0], at(a, b0, c0))

    def reduce_step(t, carry):
        @pl.when(t < A)
        def _():
            a = turn(a0, t + 1, A)
            done = None
            for i, (blk, copy) in enumerate(first(a)):
                if i % 2 == 0:
                    part[blk] = product(blk).astype(BF16)
                copy.start()

        @pl.when(jnp.logical_and(t >= 1, t < A + 1))
        def _():
            a = turn(a0, t, A)
            for blk, other, way, copy in second(a):
                value = product(blk)
                if way == 0:
                    edge = value[0:half]
                    for db in range(1, B):
                        b = turn(b0, db, B)
                        slot = r1y.at[a, other, b]
                        remote(slot, slot, s1y.at[blk], q1y.at[a, other, b], at(a0, b, c0)).wait_recv()
                        edge = edge + r1y[a, other, b].astype(F32)
                    part[blk, 0:half] = edge.astype(BF16)
                    part[blk, half:rp] = value[half:rp].astype(BF16)
                else:
                    edge = value[half:rp]
                    for dc in range(1, C):
                        c = turn(c0, dc, C)
                        slot = r1x.at[a, other, c]
                        remote(slot, slot, s1x.at[blk], q1x.at[a, other, c], at(a0, b0, c)).wait_recv()
                        edge = edge + r1x[a, other, c].astype(F32)
                    part[blk, 0:half] = value[0:half].astype(BF16)
                    part[blk, half:rp] = edge.astype(BF16)
                copy.start()

        @pl.when(t >= 2)
        def _():
            a = turn(a0, t - 1, A)
            blk = at(a, b0, c0)
            value = product(blk)
            for dc in range(1, C):
                c = turn(c0, dc, C)
                slot = r2x.at[a, c]
                remote(slot, slot, s2.at[blk], q2x.at[a, c], at(a0, b0, c)).wait_recv()
                value = value + r2x[a, c].astype(F32)
            for db in range(1, B):
                b = turn(b0, db, B)
                slot = r2y.at[a, b]
                remote(slot, slot, s2.at[blk], q2y.at[a, b], at(a0, b, c0)).wait_recv()
                value = value + r2y[a, b].astype(F32)
            sums[...] = value

            @pl.when(t < A + 1)
            def _():
                part[blk] = value.astype(BF16)
                third(a).start()

        return carry

    lax.fori_loop(0, A + 2, reduce_step, 0)

    loads[2].wait()
    for b in range(n):
        emb3[b] = emb_v[:, b * dl:(b + 1) * dl]

    proj = to_column(stat_sum(1, st_pr), 128)
    share = sums[...]
    for da in range(1, A):
        a = turn(a0, da, A)
        remote(r3.at[a], r3.at[a], s3.at[a], q3.at[a], at(a, b0, c0)).wait_recv()
        share = share + r3[a].astype(F32)
    inv = inv_ref[0:rows, 0:1]
    scaled = share[0:rows] * gain3[me]
    grad = cot_in[...].astype(F32) + inv * scaled - x_own * (inv * inv * (proj[0:rows, 0:1] / width))
    gg[me] = jnp.zeros((rp, dl), BF16)
    gg[me, 0:rows, :] = grad.astype(BF16)

    def settle(d, carry):
        a = turn(a0, d, A)
        for _, copy in first(a):
            copy.wait_send()
        for _, _, _, copy in second(a):
            copy.wait_send()

        @pl.when(d >= 1)
        def _():
            third(a).wait_send()

        return carry

    def score(blk):
        scores[...] += lax.dot_general(gg[blk], emb3[blk], NT, preferred_element_type=F32)

    gather(gg, g_send, g_recv, lambda: None, score)
    lax.fori_loop(0, A, settle, 0)

    def member_copy(d):
        return remote(scores, others.at[mine], m_send.at[d], m_recv.at[mine],
                      turn(mine, d, members), "member")

    for d in range(1, members):
        member_copy(d).start()
    ids = to_column(first_row(rp)[:, 0:rows] * ids_in[...].astype(F32), vl)
    entry = (lax.broadcasted_iota(jnp.int32, (rows, vl), 1) + me * vl).astype(F32)
    total = scores[...]
    for d in range(1, members):
        src = turn(mine, d, members)
        remote(others.at[src], others.at[src], m_send.at[d], m_recv.at[src], src, "member").wait_recv()
        total = total + others[src]
    own = jnp.where(ids == entry, total[0:rows], 0.0)
    st_in[2] = to_row(jnp.concatenate([own, jnp.zeros((rp - rows, vl), F32)], axis=0))
    stat_send(2, st_cu)
    current = to_column(stat_sum(2, st_cu), 128)
    out_ref[...] = total[0:rows] - current[0:rows, 0:1]
    for d in range(1, members):
        member_copy(d).wait_send()


def on_device(n, members, layer_input, norm_gain, w_gate, w_up, hidden_cot, output_cot, embed, suffix_ids):
    _, rows, dl = layer_input.shape
    width = norm_gain.shape[1]
    fl = w_gate.shape[2]
    vl = embed.shape[1]
    lines = A, B, C = grid_of(n)
    rp = -(-rows // 32) * 32
    fp = -(-fl // 128) * 128
    half = rp // 2
    per = (B - 1) + (C - 1) + 2 * (B - 1) * (C - 1)
    moves = (A - 1) + A * per
    vmem = pl.BlockSpec(memory_space=pltpu.VMEM)
    hbm = pl.BlockSpec(memory_space=pl.ANY)
    dma = pltpu.SemaphoreType.DMA
    V = pltpu.VMEM
    scratch = [
        V((n, rp, dl), BF16), V((n, rp, dl), BF16), V((n, rp, dl), BF16),
        V((A, C, B, half, dl), BF16), V((A, B, C, half, dl), BF16),
        V((A, C, rp, dl), BF16), V((A, B, rp, dl), BF16), V((A, rp, dl), BF16),
        V((3, 8, rp), F32), V((n, 8, rp), F32), V((n, 8, rp), F32), V((n, 8, rp), F32),
        V((width, fl), BF16), V((width, fl), BF16), V((width, 2 * fp), BF16),
        V((vl, width), BF16), V((n, vl, dl), BF16), V((n, 1, dl), F32),
        V((rp, 2 * fp), BF16), V((rp, 2 * fp), F32), V((rp, 128), F32), V((rp, dl), F32),
        V((rp, vl), F32), V((members, rp, vl), F32),
        dma((3,)), dma((3, n)), dma((3, n)), dma((moves,)), dma((n, 2)), dma((moves,)), dma((n, 2)),
        dma((n,)), dma((A, C, B)), dma((n,)), dma((A, B, C)), dma((n,)), dma((A, C)), dma((A, B)),
        dma((A,)), dma((A,)), dma((members,)), dma((members,)),
    ]
    return pl.pallas_call(
        functools.partial(kernel, n, members, lines, rows, width),
        out_shape=jax.ShapeDtypeStruct((rows, vl), F32),
        in_specs=[vmem] * 5 + [hbm] * 3,
        out_specs=vmem,
        scratch_shapes=scratch,
        compiler_params=pltpu.CompilerParams(
            collective_id=0, has_side_effects=True, vmem_limit_bytes=56 * 1024 * 1024
        ),
    )(layer_input[0], norm_gain, hidden_cot[0], output_cot[0], suffix_ids[None, :],
      w_gate[0], w_up[0], embed[0])


def solution(mesh):
    n, members = mesh.shape["shard"], mesh.shape["member"]
    placed = (
        P("member", None, "shard"),
        P("member", None),
        P("member", None, "shard"),
        P("member", None, "shard"),
        P("member", None, "shard"),
        P("member", None, "shard"),
        P("member", "shard", None),
        P(),
    )
    return jax.shard_map(
        functools.partial(on_device, n, members),
        mesh=mesh, in_specs=placed, out_specs=P(None, "shard"), check_vma=False,
    )
```

time: 418 us -> 108 us (0.26)
  waiting for transfers between devices: 274 us -> 0 us
  Pallas kernels: 0 us -> 102 us
  blocking collectives: 80.5 us -> 0 us
  local copies, waits for them, and re-layouts: 29.3 us -> 5.55 us
  matrix products: 15.9 us -> 0 us
  between operations: 13.2 us -> 0.01 us
    all_gather x2 -> x0, waiting for transfers between devices: 146 us -> none  [the longest x1 88.6 us: on_device(): whole_input = lax.all_gather(input_local, 'shard', axis=1, tiled=True)]
    unnamed x5 -> x0, waiting for transfers between devices: 114 us -> none
    pallas_call x0 -> x1, Pallas kernels: none -> 102 us  [on_device(): pl.pallas_call(functools.partial(kernel, n, members, lines, rows, width),...]
    psum x2 -> x0, blocking collectives: 80.5 us -> none  [the longest x1 41.3 us: on_device(): proj = lax.psum(partial_proj, 'shard')[:, None] / width]
    dot_general x4 -> x0, matrix products: 15.9 us -> none  [the longest x1 6.23 us: on_device(): lax.dot_general(gate_w, gate_grad, contract, preferred_element_type=jnp.f...]
    all_gather x2 -> x0, local copies, waits for them, and re-layouts: 14.3 us -> none  [the longest x1 11 us: on_device(): whole_input = lax.all_gather(input_local, 'shard', axis=1, tiled=True)]
    psum x1 -> x0, waiting for transfers between devices: 14.1 us -> none  [on_device(): delta = lax.psum(scores - current[:, None], 'member')]
    unnamed x19 -> x5, local copies, waits for them, and re-layouts: 14.9 us -> 5.55 us
  transfers between devices with their start and end apart: 4 -> 0, of which waited for: 4 -> 0; matrix products, arithmetic and copies ran while one was open for 0% -> 0% of each run, Pallas kernels for 0% -> 0%
where the time goes in v1:
time: 108 us; the launch traced here: 107 us
  Pallas kernels  102 us (94%)
  local copies, waits for them, and re-layouts  5.55 us (5%)
    pallas_call x1, Pallas kernels, on_device(): pl.pallas_call(functools.partial(kernel, n, members, lines, rows, width),...  102 us
    unnamed x5, local copies, waits for them, and re-layouts  5.55 us

profile of v1, /device:TPU:0, one launch (start us, length us, event | category | flops | bytes accessed | tf_op | source)
XLA Modules:
  0.0 107.2 jit_solution(2633604811217433174)
XLA Ops:
  0.0 0.0 copy-start
  0.0 2.5 %copy.9 = bf16[1,5120,112]{2,1,0:T(8,128)(2,1)} copy(bf16[1,5120,112]{1,2,0:T(8,128)(2,1)} %param.10) | data formatting | bytes 2293760 | tf_op args[2]
  2.5 0.0 copy-done
  2.5 1.4 %copy.10 = bf16[1,5120,112]{2,1,0:T(8,128)(2,1)} copy(bf16[1,5120,112]{1,2,0:T(8,128)(2,1)S(1)} %copy-done) | data formatting | bytes 2293760 | tf_op args[3]
  3.9 101.6 %shard_map.82 = f32[180,256]{1,0:T(8,128)} custom-call(bf16[180,320]{1,0:T(8,128)(2,1)} %bitcast.10, f32[1,5120]{1,0:T(1,128)} %gain_in.1, bf16[180,112]{1,0:T(8,128)(2,1)} %bitcast.12, bf16[180,320]{1,0:T(8,128)(2,1)} %bitcast.11, s32[1,180]{1,0:T(1,128)} %bitcast.13, bf16[5120,112]{1,0:T(8,128)(2,1)} %bitcast.7, bf16[5120,112]{1,0:T(8,128)(2,1)} %bitcast.8, ...), custom_call_target="tpu_custom_call" | custom-call | tf_op jit(solution)/shard_map/pallas_call | solution.py:418
  105.6 1.6 %copy.12 = f32[180,256]{1,0:T(8,128)} copy(f32[180,256]{1,0:T(8,128)} %shard_map.82) | data formatting | bytes 368640
Async XLA Ops:
  0.0 2.5 %copy-start = (bf16[1,5120,112]{1,2,0:T(8,128)(2,1)S(1)}, bf16[1,5120,112]{1,2,0:T(8,128)(2,1)}, u32[]{:S(2)}) copy-start(bf16[1,5120,112]{1,2,0:T(8,128)(2,1)} %param.11) | copy-start | bytes 3440644

commit v2 on v1

--- a/solution.py
+++ b/solution.py
@@ -21,19 +21,47 @@
     return n // (inner * inner), inner, inner
 
 
+def pack(value):
+    rp, dl = value.shape
+    q, r = divmod(dl, 128)
+    pieces = [value[:, k * 128:(k + 1) * 128] for k in range(q)]
+    if r:
+        tail = value[:, q * 128:]
+        if r <= 64:
+            tail = jnp.concatenate([tail, jnp.zeros((rp, 64 - r), tail.dtype)], axis=1) if r < 64 else tail
+            tail = jnp.concatenate([tail[:rp // 2], tail[rp // 2:]], axis=1)
+        else:
+            tail = jnp.concatenate([tail, jnp.zeros((rp, 128 - r), tail.dtype)], axis=1)
+        pieces.append(tail)
+    return jnp.concatenate(pieces, axis=0) if len(pieces) > 1 else pieces[0]
+
+
+def unpack(packed, rp, dl):
+    q, r = divmod(dl, 128)
+    pieces = [packed[k * rp:(k + 1) * rp] for k in range(q)]
+    if r:
+        tail = packed[q * rp:]
+        if r <= 64:
+            tail = jnp.concatenate([tail[:, :r], tail[:, 64:64 + r]], axis=0)
+        else:
+            tail = tail[:, :r]
+        pieces.append(tail)
+    return jnp.concatenate(pieces, axis=1) if len(pieces) > 1 else pieces[0]
+
+
 def kernel(
     n, members, lines, rows, width,
-    x_in, gain_in, hid_in, cot_in, ids_in, wg_hbm, wu_hbm, emb_hbm, out_ref,
+    x_in, gain_in, hid_in, cot_in, ids_in, wg_hbm, wu_hbm, emb_hbm, out_ref, cur_ref,
     xg, gg, part, r1y, r1x, r2x, r2y, r3, st_in, st_sq, st_pr, st_cu,
-    wg_v, wu_v, wcat, emb_v, emb3, gain3, hcat, acc, inv_ref, sums, scores, others,
+    wg_v, wu_v, wt3, emb_v, emb3, gain3, hcat, acc, inv_ref, sums, scores, others,
     load_sem, st_send, st_recv, x_send, x_recv, g_send, g_recv,
     s1y, q1y, s1x, q1x, s2, q2x, q2y, s3, q3, m_send, m_recv,
 ):
     A, B, C = lines
-    rp, dl = xg.shape[1], xg.shape[2]
-    half = rp // 2
+    dl = x_in.shape[1]
+    rp = hcat.shape[0]
+    half = xg.shape[1] // 2
     fl = hid_in.shape[1]
-    fp = hcat.shape[1] // 2
     vl = emb_hbm.shape[0]
     me = lax.axis_index("shard")
     mine = lax.axis_index("member")
@@ -45,7 +73,13 @@
         return (a * B + b) * C + c
 
     def turn(v, d, size):
-        return lax.rem(v + d, size)
+        if size & (size - 1):
+            return lax.rem(v + d, size)
+        for k in range(size.bit_length() - 1):
+            bit = 2 ** k
+            on = (d // bit) % 2 if isinstance(d, int) else lax.rem(lax.div(d, bit), 2)
+            v = v + on * (bit - 2 * bit * lax.rem(lax.div(v, bit), 2))
+        return v
 
     def remote(src, dst, send, recv, peer, axis="shard"):
         return pltpu.make_async_remote_copy(
@@ -69,9 +103,9 @@
         pl.semaphore_signal(barrier, inc=1, device_id={"member": turn(mine, d, members)},
                             device_id_type=pl.DeviceIdType.MESH)
 
-    xg[me] = jnp.zeros((rp, dl), BF16)
-    xg[me, 0:rows, :] = x_in[...]
-    x_own = x_in[...].astype(F32)
+    pad = jnp.zeros((rp - rows, dl), F32)
+    x_own = jnp.concatenate([x_in[...].astype(F32), pad], axis=0)
+    xg[me] = pack(x_own).astype(BF16)
 
     def first_row(k):
         return (lax.broadcasted_iota(jnp.int32, (8, k), 0) == 0).astype(F32)
@@ -101,8 +135,7 @@
             stat_copy(k, buf, d).wait_send()
         return total
 
-    pad = jnp.zeros((rp - rows, dl), F32)
-    st_in[0] = to_row(jnp.concatenate([x_own * x_own, pad], axis=0))
+    st_in[0] = to_row(x_own * x_own)
     pl.semaphore_wait(barrier, n - 1 + members - 1)
 
     def gather(buf, send, recv, before, process):
@@ -203,39 +236,37 @@
     def prepare():
         for b in range(n):
             gain3[b] = gain_in[:, b * dl:(b + 1) * dl]
-        wcat[...] = jnp.zeros_like(wcat)
         loads[0].wait()
-        wcat[:, 0:fl] = wg_v[...]
         loads[1].wait()
-        wcat[:, fp:fp + fl] = wu_v[...]
+        for b in range(n):
+            wt3[b, 0:fl] = wg_v[:, b * dl:(b + 1) * dl]
+            wt3[b, fl:2 * fl] = wu_v[:, b * dl:(b + 1) * dl]
         acc[...] = jnp.zeros_like(acc)
         scores[...] = jnp.zeros_like(scores)
         square = to_column(stat_sum(0, st_sq), 128)
         inv_ref[...] = 1.0 / jnp.sqrt(square / width + 1e-05)
 
     def up(blk):
-        x = xg[blk].astype(F32)
+        x = unpack(xg[blk].astype(F32), rp, dl)
         normed = (x * inv_ref[:, 0:1] * gain3[blk]).astype(BF16)
-        w = wcat[pl.ds(pl.multiple_of(blk * dl, dl), dl), :]
-        acc[...] += jnp.dot(normed, w, preferred_element_type=F32)
+        acc[...] += lax.dot_general(normed, wt3[blk], NT, preferred_element_type=F32)
 
     gather(xg, x_send, x_recv, prepare, up)
 
     gate_pre = acc[0:rows, 0:fl]
-    up_proj = acc[0:rows, fp:fp + fl]
+    up_proj = acc[0:rows, fl:2 * fl]
     hid = hid_in[...].astype(F32)
     s = jax.nn.sigmoid(gate_pre)
     gate_grad = (hid * up_proj * s * (1.0 + gate_pre * (1.0 - s))).astype(BF16)
     up_grad = (hid * gate_pre * s).astype(BF16)
     hcat[...] = jnp.zeros_like(hcat)
     hcat[0:rows, 0:fl] = gate_grad
-    hcat[0:rows, fp:fp + fl] = up_grad
+    hcat[0:rows, fl:2 * fl] = up_grad
     st_in[1] = to_row(hcat[...].astype(F32) * acc[...])
     stat_send(1, st_pr)
 
     def product(blk):
-        w = wcat[pl.ds(pl.multiple_of(blk * dl, dl), dl), :]
-        return lax.dot_general(hcat[...], w, NT, preferred_element_type=F32)
+        return pack(jnp.dot(hcat[...], wt3[blk], preferred_element_type=F32))
 
     lo, hi = pl.ds(0, half), pl.ds(half, half)
 
@@ -272,8 +303,7 @@
     def reduce_step(t, carry):
         @pl.when(t < A)
         def _():
-            a = turn(a0, t + 1, A)
-            done = None
+            a = turn(a0, lax.rem(t + 1, A), A)
             for i, (blk, copy) in enumerate(first(a)):
                 if i % 2 == 0:
                     part[blk] = product(blk).astype(BF16)
@@ -281,7 +311,7 @@
 
         @pl.when(jnp.logical_and(t >= 1, t < A + 1))
         def _():
-            a = turn(a0, t, A)
+            a = turn(a0, lax.rem(t, A), A)
             for blk, other, way, copy in second(a):
                 value = product(blk)
                 if way == 0:
@@ -292,16 +322,16 @@
                         remote(slot, slot, s1y.at[blk], q1y.at[a, other, b], at(a0, b, c0)).wait_recv()
                         edge = edge + r1y[a, other, b].astype(F32)
                     part[blk, 0:half] = edge.astype(BF16)
-                    part[blk, half:rp] = value[half:rp].astype(BF16)
+                    part[blk, half:] = value[half:].astype(BF16)
                 else:
-                    edge = value[half:rp]
+                    edge = value[half:]
                     for dc in range(1, C):
                         c = turn(c0, dc, C)
                         slot = r1x.at[a, other, c]
                         remote(slot, slot, s1x.at[blk], q1x.at[a, other, c], at(a0, b0, c)).wait_recv()
                         edge = edge + r1x[a, other, c].astype(F32)
                     part[blk, 0:half] = value[0:half].astype(BF16)
-                    part[blk, half:rp] = edge.astype(BF16)
+                    part[blk, half:] = edge.astype(BF16)
                 copy.start()
 
         @pl.when(t >= 2)
@@ -340,11 +370,11 @@
         a = turn(a0, da, A)
         remote(r3.at[a], r3.at[a], s3.at[a], q3.at[a], at(a, b0, c0)).wait_recv()
         share = share + r3[a].astype(F32)
-    inv = inv_ref[0:rows, 0:1]
-    scaled = share[0:rows] * gain3[me]
-    grad = cot_in[...].astype(F32) + inv * scaled - x_own * (inv * inv * (proj[0:rows, 0:1] / width))
-    gg[me] = jnp.zeros((rp, dl), BF16)
-    gg[me, 0:rows, :] = grad.astype(BF16)
+    inv = inv_ref[:, 0:1]
+    scaled = unpack(share, rp, dl) * gain3[me]
+    cot = jnp.concatenate([cot_in[...].astype(F32), pad], axis=0)
+    grad = cot + inv * scaled - x_own * (inv * inv * (proj[:, 0:1] / width))
+    gg[me] = pack(grad).astype(BF16)
 
     def settle(d, carry):
         a = turn(a0, d, A)
@@ -360,7 +390,7 @@
         return carry
 
     def score(blk):
-        scores[...] += lax.dot_general(gg[blk], emb3[blk], NT, preferred_element_type=F32)
+        scores[...] += lax.dot_general(unpack(gg[blk], rp, dl), emb3[blk], NT, preferred_element_type=F32)
 
     gather(gg, g_send, g_recv, lambda: None, score)
     lax.fori_loop(0, A, settle, 0)
@@ -382,7 +412,8 @@
     st_in[2] = to_row(jnp.concatenate([own, jnp.zeros((rp - rows, vl), F32)], axis=0))
     stat_send(2, st_cu)
     current = to_column(stat_sum(2, st_cu), 128)
-    out_ref[...] = total[0:rows] - current[0:rows, 0:1]
+    out_ref[...] = total[0:rows]
+    cur_ref[...] = current[0:rows]
     for d in range(1, members):
         member_copy(d).wait_send()
 
@@ -394,8 +425,9 @@
     vl = embed.shape[1]
     lines = A, B, C = grid_of(n)
     rp = -(-rows // 32) * 32
-    fp = -(-fl // 128) * 128
-    half = rp // 2
+    q, r = divmod(dl, 128)
+    length = q * rp + (0 if r == 0 else rp // 2 if r <= 64 else rp)
+    half = length // 2
     per = (B - 1) + (C - 1) + 2 * (B - 1) * (C - 1)
     moves = (A - 1) + A * per
     vmem = pl.BlockSpec(memory_space=pltpu.VMEM)
@@ -403,29 +435,30 @@
     dma = pltpu.SemaphoreType.DMA
     V = pltpu.VMEM
     scratch = [
-        V((n, rp, dl), BF16), V((n, rp, dl), BF16), V((n, rp, dl), BF16),
-        V((A, C, B, half, dl), BF16), V((A, B, C, half, dl), BF16),
-        V((A, C, rp, dl), BF16), V((A, B, rp, dl), BF16), V((A, rp, dl), BF16),
+        V((n, length, 128), BF16), V((n, length, 128), BF16), V((n, length, 128), BF16),
+        V((A, C, B, half, 128), BF16), V((A, B, C, half, 128), BF16),
+        V((A, C, length, 128), BF16), V((A, B, length, 128), BF16), V((A, length, 128), BF16),
         V((3, 8, rp), F32), V((n, 8, rp), F32), V((n, 8, rp), F32), V((n, 8, rp), F32),
-        V((width, fl), BF16), V((width, fl), BF16), V((width, 2 * fp), BF16),
+        V((fl, width), BF16), V((fl, width), BF16), V((n, 2 * fl, dl), BF16),
         V((vl, width), BF16), V((n, vl, dl), BF16), V((n, 1, dl), F32),
-        V((rp, 2 * fp), BF16), V((rp, 2 * fp), F32), V((rp, 128), F32), V((rp, dl), F32),
+        V((rp, 2 * fl), BF16), V((rp, 2 * fl), F32), V((rp, 128), F32), V((length, 128), F32),
         V((rp, vl), F32), V((members, rp, vl), F32),
         dma((3,)), dma((3, n)), dma((3, n)), dma((moves,)), dma((n, 2)), dma((moves,)), dma((n, 2)),
         dma((n,)), dma((A, C, B)), dma((n,)), dma((A, B, C)), dma((n,)), dma((A, C)), dma((A, B)),
         dma((A,)), dma((A,)), dma((members,)), dma((members,)),
     ]
-    return pl.pallas_call(
+    total, current = pl.pallas_call(
         functools.partial(kernel, n, members, lines, rows, width),
-        out_shape=jax.ShapeDtypeStruct((rows, vl), F32),
+        out_shape=(jax.ShapeDtypeStruct((rows, vl), F32), jax.ShapeDtypeStruct((rows, 128), F32)),
         in_specs=[vmem] * 5 + [hbm] * 3,
-        out_specs=vmem,
+        out_specs=(vmem, vmem),
         scratch_shapes=scratch,
         compiler_params=pltpu.CompilerParams(
             collective_id=0, has_side_effects=True, vmem_limit_bytes=56 * 1024 * 1024
         ),
     )(layer_input[0], norm_gain, hidden_cot[0], output_cot[0], suffix_ids[None, :],
-      w_gate[0], w_up[0], embed[0])
+      w_gate[0].T, w_up[0].T, embed[0])
+    return total - current[:, 0:1]
 
 
 def solution(mesh):

time: 108 us -> 89.9 us (0.83)
  Pallas kernels: 102 us -> 87 us
  local copies, waits for them, and re-layouts: 5.55 us -> 0.99 us
  other arithmetic: 0 us -> 1.7 us
    pallas_call x1, Pallas kernels: 102 us -> 87 us  [on_device(): pl.pallas_call(functools.partial(kernel, n, members, lines, rows, width),...]
    unnamed x5 -> x0, local copies, waits for them, and re-layouts: 5.55 us -> none
    sub x0 -> x1, other arithmetic: none -> 1.7 us  [on_device(): return total - current[:, 0:1]]
where the time goes in v2:
time: 89.9 us; the launch traced here: 89.7 us
  Pallas kernels  87 us (97%)
  other arithmetic  1.7 us (2%)
  local copies, waits for them, and re-layouts  0.99 us (1%)
    pallas_call x1, Pallas kernels, on_device(): pl.pallas_call(functools.partial(kernel, n, members, lines, rows, width),...  87 us

profile of v2, /device:TPU:0, one launch (start us, length us, event | category | flops | bytes accessed | tf_op | source)
XLA Modules:
  0.0 89.7 jit_solution(6936143567861513521)
XLA Ops:
  0.0 87.0 %shard_map.82 = (f32[180,256]{1,0:T(8,128)}, f32[180,128]{1,0:T(8,128)}) custom-call(bf16[180,320]{1,0:T(8,128)(2,1)} %bitcast.14, f32[1,5120]{1,0:T(1,128)} %gain_in.1, bf16[180,112]{1,0:T(8,128)(2,1)} %bitcast.16, bf16[180,320]{1,0:T(8,128)(2,1)} %bitcast.15, s32[1,180]{1,0:T(1,128)} %bitcast.17, bf16[112,5120]{1,0:T(8,128)(2,1)} %bitcast.12, ...), custom_call_target="tpu_custom_call" | custom-call | tf_op jit(solution)/shard_map/pallas_call | solution.py:450
  87.0 1.0 %slice_reduce_fusion = f32[180]{0:T(256)S(1)} fusion(f32[180,128]{1,0:T(8,128)} %get-tuple-element.8), kind=kLoop, calls=%fused_computation.1 | loop fusion | bytes 1440 | tf_op jit(solution)/shard_map/slice | solution.py:461
  88.0 1.7 %broadcast_subtract_fusion = f32[180,256]{1,0:T(8,128)} fusion(f32[180,256]{1,0:T(8,128)} %get-tuple-element.7, f32[180]{0:T(256)S(1)} %slice_reduce_fusion), kind=kLoop, calls=%fused_computation | loop fusion | flops 46080 | bytes 369360 | tf_op jit(solution)/shard_map/sub | solution.py:461

commit v3 on v2

--- a/solution.py
+++ b/solution.py
@@ -51,9 +51,9 @@
 
 def kernel(
     n, members, lines, rows, width,
-    x_in, gain_in, hid_in, cot_in, ids_in, wg_hbm, wu_hbm, emb_hbm, out_ref, cur_ref,
+    x_in, gain_in, hid_in, cot_in, ids_in, wg_hbm, wu_hbm, emb_hbm, out_ref,
     xg, gg, part, r1y, r1x, r2x, r2y, r3, st_in, st_sq, st_pr, st_cu,
-    wg_v, wu_v, wt3, emb_v, emb3, gain3, hcat, acc, inv_ref, sums, scores, others,
+    wg_v, wu_v, wt3, emb_v, emb3, gain3, hcat, acc, inv_ref, sums, kept, scores, others,
     load_sem, st_send, st_recv, x_send, x_recv, g_send, g_recv,
     s1y, q1y, s1x, q1x, s2, q2x, q2y, s3, q3, m_send, m_recv,
 ):
@@ -112,10 +112,11 @@
 
     def to_row(values):
         return lax.dot_general(first_row(values.shape[1]), values, NT, precision=HIGH,
-                               preferred_element_type=F32)
+                               preferred_element_type=F32)[0:1]
 
     def to_column(row, lanes):
-        return lax.dot_general(row, jnp.ones((8, lanes), F32), TN, precision=HIGH,
+        rows8 = first_row(row.shape[1]) * row
+        return lax.dot_general(rows8, jnp.ones((8, lanes), F32), TN, precision=HIGH,
                                preferred_element_type=F32)
 
     def stat_copy(k, buf, d):
@@ -139,81 +140,90 @@
     pl.semaphore_wait(barrier, n - 1 + members - 1)
 
     def gather(buf, send, recv, before, process):
-        per = (B - 1) + (C - 1) + 2 * (B - 1) * (C - 1)
-
-        def line(blk, index, peer):
-            return remote(buf.at[blk], buf.at[blk], send.at[index], recv.at[blk, 0], peer)
-
-        def piece(blk, index, peer, h):
+        per = 2 * (B - 1) + 2 * (C - 1) + 2 * (B - 1) * (C - 1)
+
+        def piece(blk, h, index, peer):
             view = buf.at[blk, pl.ds(h * half, half)]
             return remote(view, view, send.at[index], recv.at[blk, h], peer)
 
         def outs(da):
             a = turn(a0, da, A)
-            base = (A - 1) + da * per
-            full, low, high = [], [], []
+            base = 2 * (A - 1) + da * per
+            full, low, high = ([], []), [], []
             k = 0
-            for db in range(1, B):
-                full.append(line(at(a, b0, c0), base + k, at(a0, turn(b0, db, B), c0)))
-                k += 1
-            for dc in range(1, C):
-                full.append(line(at(a, b0, c0), base + k, at(a0, b0, turn(c0, dc, C))))
-                k += 1
+            for h in (0, 1):
+                for dc in range(1, C):
+                    full[h].append(piece(at(a, b0, c0), h, base + k, at(a0, b0, turn(c0, dc, C))))
+                    k += 1
+                for db in range(1, B):
+                    full[h].append(piece(at(a, b0, c0), h, base + k, at(a0, turn(b0, db, B), c0)))
+                    k += 1
             for dc in range(1, C):
                 for db in range(1, B):
-                    low.append(piece(at(a, b0, turn(c0, dc, C)), base + k,
-                                     at(a0, turn(b0, db, B), c0), 0))
+                    low.append(piece(at(a, b0, turn(c0, dc, C)), 0, base + k,
+                                     at(a0, turn(b0, db, B), c0)))
                     k += 1
             for db in range(1, B):
                 for dc in range(1, C):
-                    high.append(piece(at(a, turn(b0, db, B), c0), base + k,
-                                      at(a0, b0, turn(c0, dc, C)), 1))
+                    high.append(piece(at(a, turn(b0, db, B), c0), 1, base + k,
+                                      at(a0, b0, turn(c0, dc, C))))
                     k += 1
             return full, low, high
 
-        def outer(da):
-            return line(me, da - 1, at(turn(a0, da, A), b0, c0))
-
-        for copy in outs(0)[0]:
-            copy.start()
+        def outer(da, h):
+            return piece(me, h, 2 * (da - 1) + h, at(turn(a0, da, A), b0, c0))
+
+        own = outs(0)[0]
+        for h in (0, 1):
+            for copy in own[h][:C - 1] + own[1 - h][C - 1:]:
+                copy.start()
         for da in range(1, A):
-            outer(da).start()
+            for h in (0, 1):
+                outer(da, h).start()
         before()
 
         def step(t, carry):
             @pl.when(jnp.logical_and(t >= 1, t < A))
             def _():
                 src = at(turn(a0, t, A), b0, c0)
-                line(src, 0, src).wait_recv()
-                for copy in outs(t)[0]:
-                    copy.start()
+                full = outs(t)[0]
+                for h in (0, 1):
+                    piece(src, h, 0, src).wait_recv()
+                    for copy in full[h]:
+                        copy.start()
 
             @pl.when(jnp.logical_and(t >= 1, t < A + 1))
             def _():
-                da = t - 1
-                a = turn(a0, da, A)
-                _, low, high = outs(da)
-                xs = [at(a, b0, turn(c0, dc, C)) for dc in range(1, C)]
-                ys = [at(a, turn(b0, db, B), c0) for db in range(1, B)]
-                for i, blk in enumerate(xs):
-                    line(blk, 0, at(a0, b0, turn(c0, i + 1, C))).wait_recv()
+                a = turn(a0, t - 1, A)
+                _, low, high = outs(t - 1)
+                for i in range(C - 1):
+                    c = turn(c0, i + 1, C)
+                    piece(at(a, b0, c), 0, 0, at(a0, b0, c)).wait_recv()
                     for copy in low[i * (B - 1):(i + 1) * (B - 1)]:
                         copy.start()
-                for i, blk in enumerate(ys):
-                    line(blk, 0, at(a0, turn(b0, i + 1, B), c0)).wait_recv()
+                for i in range(B - 1):
+                    b = turn(b0, i + 1, B)
+                    piece(at(a, b, c0), 1, 0, at(a0, b, c0)).wait_recv()
                     for copy in high[i * (C - 1):(i + 1) * (C - 1)]:
                         copy.start()
-                for blk in [at(a, b0, c0)] + xs + ys:
-                    process(blk)
+                process(at(a, b0, c0))
 
             @pl.when(t >= 2)
             def _():
                 a = turn(a0, t - 2, A)
+                for dc in range(1, C):
+                    c = turn(c0, dc, C)
+                    piece(at(a, b0, c), 1, 0, at(a0, b0, c)).wait_recv()
+                    process(at(a, b0, c))
+                for db in range(1, B):
+                    b = turn(b0, db, B)
+                    piece(at(a, b, c0), 0, 0, at(a0, b, c0)).wait_recv()
+                    process(at(a, b, c0))
                 for db in range(1, B):
                     for dc in range(1, C):
                         b, c = turn(b0, db, B), turn(c0, dc, C)
-                        piece(at(a, b, c), 0, at(a0, b, c0), 0).wait_recv()
-                        piece(at(a, b, c), 0, at(a0, b0, c), 1).wait_recv()
+                        piece(at(a, b, c), 0, 0, at(a0, b, c0)).wait_recv()
+                        piece(at(a, b, c), 1, 0, at(a0, b0, c)).wait_recv()
                         process(at(a, b, c))
 
             return carry
@@ -221,11 +231,12 @@
         lax.fori_loop(0, A + 2, step, 0)
 
         for da in range(1, A):
-            outer(da).wait_send()
+            for h in (0, 1):
+                outer(da, h).wait_send()
 
         def done(da, carry):
             full, low, high = outs(da)
-            for copy in full + low + high:
+            for copy in full[0] + full[1] + low + high:
                 copy.wait_send()
             return carry
 
@@ -287,18 +298,21 @@
         for dc in range(1, C):
             c = turn(c0, dc, C)
             blk = at(a, b0, c)
-            copies.append((blk, c, 0, remote(part.at[blk], r2x.at[a, c0], s2.at[blk],
-                                             q2x.at[a, c0], at(a0, b0, c))))
+            pair = [remote(part.at[blk, span], r2x.at[a, c0, span], s2.at[blk, h],
+                           q2x.at[a, c0, h], at(a0, b0, c)) for h, span in ((1, hi), (0, lo))]
+            copies.append((blk, c, 0, pair))
         for db in range(1, B):
             b = turn(b0, db, B)
             blk = at(a, b, c0)
-            copies.append((blk, b, 1, remote(part.at[blk], r2y.at[a, b0], s2.at[blk],
-                                             q2y.at[a, b0], at(a0, b, c0))))
+            pair = [remote(part.at[blk, span], r2y.at[a, b0, span], s2.at[blk, h],
+                           q2y.at[a, b0, h], at(a0, b, c0)) for h, span in ((0, lo), (1, hi))]
+            copies.append((blk, b, 1, pair))
         return copies
 
-    def third(a):
+    def third(a, h):
         blk = at(a, b0, c0)
-        return remote(part.at[blk], r3.at[a0], s3.at[a], q3.at[a0], at(a, b0, c0))
+        span = (lo, hi)[h]
+        return remote(part.at[blk, span], r3.at[a0, span], s3.at[a, h], q3.at[a0, h], at(a, b0, c0))
 
     def reduce_step(t, carry):
         @pl.when(t < A)
@@ -308,53 +322,60 @@
                 if i % 2 == 0:
                     part[blk] = product(blk).astype(BF16)
                 copy.start()
+            for i, (blk, _, way, pair) in enumerate(second(a)):
+                value = product(blk)
+                if way == 0:
+                    part[blk, half:] = value[half:].astype(BF16)
+                    kept[lax.rem(t, 2), i] = value[:half]
+                else:
+                    part[blk, :half] = value[:half].astype(BF16)
+                    kept[lax.rem(t, 2), i] = value[half:]
+                pair[0].start()
 
         @pl.when(jnp.logical_and(t >= 1, t < A + 1))
         def _():
             a = turn(a0, lax.rem(t, A), A)
-            for blk, other, way, copy in second(a):
-                value = product(blk)
+            for i, (blk, other, way, pair) in enumerate(second(a)):
+                edge = kept[lax.rem(t - 1, 2), i]
                 if way == 0:
-                    edge = value[0:half]
                     for db in range(1, B):
                         b = turn(b0, db, B)
                         slot = r1y.at[a, other, b]
                         remote(slot, slot, s1y.at[blk], q1y.at[a, other, b], at(a0, b, c0)).wait_recv()
                         edge = edge + r1y[a, other, b].astype(F32)
-                    part[blk, 0:half] = edge.astype(BF16)
-                    part[blk, half:] = value[half:].astype(BF16)
+                    part[blk, :half] = edge.astype(BF16)
                 else:
-                    edge = value[half:]
                     for dc in range(1, C):
                         c = turn(c0, dc, C)
                         slot = r1x.at[a, other, c]
                         remote(slot, slot, s1x.at[blk], q1x.at[a, other, c], at(a0, b0, c)).wait_recv()
                         edge = edge + r1x[a, other, c].astype(F32)
-                    part[blk, 0:half] = value[0:half].astype(BF16)
                     part[blk, half:] = edge.astype(BF16)
-                copy.start()
+                pair[1].start()
 
         @pl.when(t >= 2)
         def _():
-            a = turn(a0, t - 1, A)
+            a = turn(a0, t - 1, A) if A & (A - 1) else turn(a0, lax.rem(t - 1, A), A)
             blk = at(a, b0, c0)
-            value = product(blk)
-            for dc in range(1, C):
-                c = turn(c0, dc, C)
-                slot = r2x.at[a, c]
-                remote(slot, slot, s2.at[blk], q2x.at[a, c], at(a0, b0, c)).wait_recv()
-                value = value + r2x[a, c].astype(F32)
-            for db in range(1, B):
-                b = turn(b0, db, B)
-                slot = r2y.at[a, b]
-                remote(slot, slot, s2.at[blk], q2y.at[a, b], at(a0, b, c0)).wait_recv()
-                value = value + r2y[a, b].astype(F32)
-            sums[...] = value
-
-            @pl.when(t < A + 1)
-            def _():
-                part[blk] = value.astype(BF16)
-                third(a).start()
+            sums[...] = product(blk)
+            for h, span in ((0, lo), (1, hi)):
+                value = sums[span]
+                for dc in range(1, C):
+                    c = turn(c0, dc, C)
+                    slot = r2x.at[a, c, span]
+                    remote(slot, slot, s2.at[blk, h], q2x.at[a, c, h], at(a0, b0, c)).wait_recv()
+                    value = value + r2x[a, c, span].astype(F32)
+                for db in range(1, B):
+                    b = turn(b0, db, B)
+                    slot = r2y.at[a, b, span]
+                    remote(slot, slot, s2.at[blk, h], q2y.at[a, b, h], at(a0, b, c0)).wait_recv()
+                    value = value + r2y[a, b, span].astype(F32)
+                sums[span] = value
+
+                @pl.when(t < A + 1)
+                def _():
+                    part[blk, span] = value.astype(BF16)
+                    third(a, h).start()
 
         return carry
 
@@ -368,7 +389,9 @@
     share = sums[...]
     for da in range(1, A):
         a = turn(a0, da, A)
-        remote(r3.at[a], r3.at[a], s3.at[a], q3.at[a], at(a, b0, c0)).wait_recv()
+        for h, span in ((0, lo), (1, hi)):
+            slot = r3.at[a, span]
+            remote(slot, slot, s3.at[a, h], q3.at[a, h], at(a, b0, c0)).wait_recv()
         share = share + r3[a].astype(F32)
     inv = inv_ref[:, 0:1]
     scaled = unpack(share, rp, dl) * gain3[me]
@@ -380,12 +403,14 @@
         a = turn(a0, d, A)
         for _, copy in first(a):
             copy.wait_send()
-        for _, _, _, copy in second(a):
-            copy.wait_send()
+        for _, _, _, pair in second(a):
+            for copy in pair:
+                copy.wait_send()
 
         @pl.when(d >= 1)
         def _():
-            third(a).wait_send()
+            third(a, 0).wait_send()
+            third(a, 1).wait_send()
 
         return carry
 
@@ -401,7 +426,7 @@
 
     for d in range(1, members):
         member_copy(d).start()
-    ids = to_column(first_row(rp)[:, 0:rows] * ids_in[...].astype(F32), vl)
+    ids = to_column(ids_in[...].astype(F32), vl)
     entry = (lax.broadcasted_iota(jnp.int32, (rows, vl), 1) + me * vl).astype(F32)
     total = scores[...]
     for d in range(1, members):
@@ -412,8 +437,7 @@
     st_in[2] = to_row(jnp.concatenate([own, jnp.zeros((rp - rows, vl), F32)], axis=0))
     stat_send(2, st_cu)
     current = to_column(stat_sum(2, st_cu), 128)
-    out_ref[...] = total[0:rows]
-    cur_ref[...] = current[0:rows]
+    out_ref[...] = total[0:rows] - current[0:rows, 0:1]
     for d in range(1, members):
         member_copy(d).wait_send()
 
@@ -428,8 +452,8 @@
     q, r = divmod(dl, 128)
     length = q * rp + (0 if r == 0 else rp // 2 if r <= 64 else rp)
     half = length // 2
-    per = (B - 1) + (C - 1) + 2 * (B - 1) * (C - 1)
-    moves = (A - 1) + A * per
+    per = 2 * (B - 1) + 2 * (C - 1) + 2 * (B - 1) * (C - 1)
+    moves = 2 * (A - 1) + A * per
     vmem = pl.BlockSpec(memory_space=pltpu.VMEM)
     hbm = pl.BlockSpec(memory_space=pl.ANY)
     dma = pltpu.SemaphoreType.DMA
@@ -438,27 +462,27 @@
         V((n, length, 128), BF16), V((n, length, 128), BF16), V((n, length, 128), BF16),
         V((A, C, B, half, 128), BF16), V((A, B, C, half, 128), BF16),
         V((A, C, length, 128), BF16), V((A, B, length, 128), BF16), V((A, length, 128), BF16),
-        V((3, 8, rp), F32), V((n, 8, rp), F32), V((n, 8, rp), F32), V((n, 8, rp), F32),
+        V((3, 1, rp), F32), V((n, 1, rp), F32), V((n, 1, rp), F32), V((n, 1, rp), F32),
         V((fl, width), BF16), V((fl, width), BF16), V((n, 2 * fl, dl), BF16),
         V((vl, width), BF16), V((n, vl, dl), BF16), V((n, 1, dl), F32),
         V((rp, 2 * fl), BF16), V((rp, 2 * fl), F32), V((rp, 128), F32), V((length, 128), F32),
+        V((2, B + C - 2, half, 128), F32),
         V((rp, vl), F32), V((members, rp, vl), F32),
         dma((3,)), dma((3, n)), dma((3, n)), dma((moves,)), dma((n, 2)), dma((moves,)), dma((n, 2)),
-        dma((n,)), dma((A, C, B)), dma((n,)), dma((A, B, C)), dma((n,)), dma((A, C)), dma((A, B)),
-        dma((A,)), dma((A,)), dma((members,)), dma((members,)),
+        dma((n,)), dma((A, C, B)), dma((n,)), dma((A, B, C)), dma((n, 2)), dma((A, C, 2)), dma((A, B, 2)),
+        dma((A, 2)), dma((A, 2)), dma((members,)), dma((members,)),
     ]
-    total, current = pl.pallas_call(
+    return pl.pallas_call(
         functools.partial(kernel, n, members, lines, rows, width),
-        out_shape=(jax.ShapeDtypeStruct((rows, vl), F32), jax.ShapeDtypeStruct((rows, 128), F32)),
+        out_shape=jax.ShapeDtypeStruct((rows, vl), F32),
         in_specs=[vmem] * 5 + [hbm] * 3,
-        out_specs=(vmem, vmem),
+        out_specs=vmem,
         scratch_shapes=scratch,
         compiler_params=pltpu.CompilerParams(
             collective_id=0, has_side_effects=True, vmem_limit_bytes=56 * 1024 * 1024
         ),
     )(layer_input[0], norm_gain, hidden_cot[0], output_cot[0], suffix_ids[None, :],
       w_gate[0].T, w_up[0].T, embed[0])
-    return total - current[:, 0:1]
 
 
 def solution(mesh):

time: 89.9 us -> 84.7 us (0.942)
  Pallas kernels: 87 us -> 83 us
  other arithmetic: 1.7 us -> 0 us
    pallas_call x1, Pallas kernels: 87 us -> 83 us  [on_device(): pl.pallas_call(functools.partial(kernel, n, members, lines, rows, width),...]
    sub x1 -> x0, other arithmetic: 1.7 us -> none  [on_device(): return total - current[:, 0:1]]
    unnamed x0 -> x1, local copies, waits for them, and re-layouts: none -> 1.61 us
    slice x1 -> x0, local copies, waits for them, and re-layouts: 0.99 us -> none  [on_device(): return total - current[:, 0:1]]
where the time goes in v3:
time: 84.7 us; the launch traced here: 84.6 us
  Pallas kernels  83 us (98%)
  local copies, waits for them, and re-layouts  1.61 us (2%)
    pallas_call x1, Pallas kernels, on_device(): pl.pallas_call(functools.partial(kernel, n, members, lines, rows, width),...  83 us

profile of v3, /device:TPU:0, one launch (start us, length us, event | category | flops | bytes accessed | tf_op | source)
XLA Modules:
  0.0 84.6 jit_solution(10760038469310378767)
XLA Ops:
  0.0 83.0 %shard_map.82 = f32[180,256]{1,0:T(8,128)} custom-call(bf16[180,320]{1,0:T(8,128)(2,1)} %bitcast.14, f32[1,5120]{1,0:T(1,128)} %gain_in.1, bf16[180,112]{1,0:T(8,128)(2,1)} %bitcast.16, bf16[180,320]{1,0:T(8,128)(2,1)} %bitcast.15, s32[1,180]{1,0:T(1,128)} %bitcast.17, bf16[112,5120]{1,0:T(8,128)(2,1)} %bitcast.12, bf16[112,5120]{1,0:T(8,128)(2,1)} %bitcast.13, ...), custom_call_target="tpu_custom_call" | custom-call | tf_op jit(solution)/shard_map/pallas_call | solution.py:475
  83.0 1.6 %copy.10 = f32[180,256]{1,0:T(8,128)} copy(f32[180,256]{1,0:T(8,128)} %shard_map.82) | data formatting | bytes 368640

commit v4 on v3

--- a/solution.py
+++ b/solution.py
@@ -137,9 +137,18 @@
         return total
 
     st_in[0] = to_row(x_own * x_own)
+    for b in range(n):
+        gain3[b] = gain_in[:, b * dl:(b + 1) * dl]
+    loads[0].wait()
+    loads[1].wait()
+    for b in range(n):
+        wt3[b, 0:fl] = wg_v[:, b * dl:(b + 1) * dl]
+        wt3[b, fl:2 * fl] = wu_v[:, b * dl:(b + 1) * dl]
+    acc[...] = jnp.zeros_like(acc)
+    scores[...] = jnp.zeros_like(scores)
     pl.semaphore_wait(barrier, n - 1 + members - 1)
 
-    def gather(buf, send, recv, before, process):
+    def gather(buf, send, recv, before, process, late):
         per = 2 * (B - 1) + 2 * (C - 1) + 2 * (B - 1) * (C - 1)
 
         def piece(blk, h, index, peer):
@@ -180,7 +189,6 @@
         for da in range(1, A):
             for h in (0, 1):
                 outer(da, h).start()
-        before()
 
         def step(t, carry):
             @pl.when(jnp.logical_and(t >= 1, t < A))
@@ -206,7 +214,16 @@
                     piece(at(a, b, c0), 1, 0, at(a0, b, c0)).wait_recv()
                     for copy in high[i * (C - 1):(i + 1) * (C - 1)]:
                         copy.start()
+
+                @pl.when(t == 1)
+                def _():
+                    before()
+
                 process(at(a, b0, c0))
+
+            @pl.when(t == A + 1)
+            def _():
+                late()
 
             @pl.when(t >= 2)
             def _():
@@ -245,15 +262,6 @@
     stat_send(0, st_sq)
 
     def prepare():
-        for b in range(n):
-            gain3[b] = gain_in[:, b * dl:(b + 1) * dl]
-        loads[0].wait()
-        loads[1].wait()
-        for b in range(n):
-            wt3[b, 0:fl] = wg_v[:, b * dl:(b + 1) * dl]
-            wt3[b, fl:2 * fl] = wu_v[:, b * dl:(b + 1) * dl]
-        acc[...] = jnp.zeros_like(acc)
-        scores[...] = jnp.zeros_like(scores)
         square = to_column(stat_sum(0, st_sq), 128)
         inv_ref[...] = 1.0 / jnp.sqrt(square / width + 1e-05)
 
@@ -262,7 +270,12 @@
         normed = (x * inv_ref[:, 0:1] * gain3[blk]).astype(BF16)
         acc[...] += lax.dot_general(normed, wt3[blk], NT, preferred_element_type=F32)
 
-    gather(xg, x_send, x_recv, prepare, up)
+    def table():
+        loads[2].wait()
+        for b in range(n):
+            emb3[b] = emb_v[:, b * dl:(b + 1) * dl]
+
+    gather(xg, x_send, x_recv, prepare, up, table)
 
     gate_pre = acc[0:rows, 0:fl]
     up_proj = acc[0:rows, fl:2 * fl]
@@ -381,10 +394,6 @@
 
     lax.fori_loop(0, A + 2, reduce_step, 0)
 
-    loads[2].wait()
-    for b in range(n):
-        emb3[b] = emb_v[:, b * dl:(b + 1) * dl]
-
     proj = to_column(stat_sum(1, st_pr), 128)
     share = sums[...]
     for da in range(1, A):
@@ -417,7 +426,7 @@
     def score(blk):
         scores[...] += lax.dot_general(unpack(gg[blk], rp, dl), emb3[blk], NT, preferred_element_type=F32)
 
-    gather(gg, g_send, g_recv, lambda: None, score)
+    gather(gg, g_send, g_recv, lambda: None, score, lambda: None)
     lax.fori_loop(0, A, settle, 0)
 
     def member_copy(d):

time: 84.7 us -> 84 us (level)
  no operation moved by 1% of the time
where the time goes in v4:
time: 84 us; the launch traced here: 83.8 us
  Pallas kernels  82.2 us (98%)
  local copies, waits for them, and re-layouts  1.61 us (2%)
    pallas_call x1, Pallas kernels, on_device(): pl.pallas_call(functools.partial(kernel, n, members, lines, rows, width),...  82.2 us

profile of v4, /device:TPU:0, one launch (start us, length us, event | category | flops | bytes accessed | tf_op | source)
XLA Modules:
  0.0 83.8 jit_solution(16951434833966481651)
XLA Ops:
  0.0 82.2 %shard_map.82 = f32[180,256]{1,0:T(8,128)} custom-call(bf16[180,320]{1,0:T(8,128)(2,1)} %bitcast.14, f32[1,5120]{1,0:T(1,128)} %gain_in.1, bf16[180,112]{1,0:T(8,128)(2,1)} %bitcast.16, bf16[180,320]{1,0:T(8,128)(2,1)} %bitcast.15, s32[1,180]{1,0:T(1,128)} %bitcast.17, bf16[112,5120]{1,0:T(8,128)(2,1)} %bitcast.12, bf16[112,5120]{1,0:T(8,128)(2,1)} %bitcast.13, ...), custom_call_target="tpu_custom_call" | custom-call | tf_op jit(solution)/shard_map/pallas_call | solution.py:484
  82.2 1.6 %copy.10 = f32[180,256]{1,0:T(8,128)} copy(f32[180,256]{1,0:T(8,128)} %shard_map.82) | data formatting | bytes 368640
